TPU v7x, 32 devices: a whole 2x2x4 slice. The times are simulated.
32 devices in a mesh: row: 4 (over z), col: 8 (over y, x, core).
Axes of the slice: x: 2, y: 2, z: 4, core: 2. Of those that a mesh axis runs over, the one named last changes fastest.
Arguments:
- inv_depth: float32 [64, 3072], P(('row', 'col')), may hold values from 0.2 to 1
- rotation: float32 [3, 64], P(None, ('row', 'col')), may hold values from -0.05 to 0.05
- translation: float32 [3, 64], P(None, ('row', 'col')), may hold values from -0.25 to 0.25
- edge_target: int32 [64, 24], P(('row', 'col')), may hold values from 0 to 63, as said below
- flow_obs: float32 [2, 64, 24, 3072], P(None, ('row', 'col')), may hold values from -2.8 to 2.8
- weight: float32 [2, 64, 24, 3072], P(None, ('row', 'col')), may hold values from 0.1 to 1
Outputs:
- depth_next: float32 [64, 3072], P(('row', 'col'))
- pose_step: float32 [6, 64], P(None, ('row', 'col'))
Inputs may be any that keep to these rules, and one draw needn't show every extreme that they name: `edge_target`: each keyframe's targets are distinct, differ from the keyframe itself, are sorted ascending, and lie in the keyframe's own block of 16 consecutive keyframes or in one of the two neighbouring blocks, the blocks counted cyclically.
All inputs are finite; a program needn't handle non-finite values.
Results may differ from a plain program's by a relative error of at most 0.0003.
Values sent between devices are 32-bit elements; how exact they have to be, the bound alone decides.
No kernel may reach another device: no remote copies, remote signals or barrier semaphores. Data moves between devices by JAX's collectives and lax.ppermute only.
A program may use at most 128 MiB of HBM per device.

v0:
```python
import jax
import jax.numpy as jnp
from jax import lax
from jax.sharding import PartitionSpec as P

IMG_H = 48
IMG_W = 64
PRECISE = lax.Precision.HIGHEST
DAMP_DEPTH = 0.1
LEVENBERG = 0.1
RIDGE = 0.001


def with_halo(cells, sides, width):
    for axis, dim in sides:
        count = lax.axis_size(axis)
        head = lax.slice_in_dim(cells, 0, width, axis=dim)
        tail = lax.slice_in_dim(cells, cells.shape[dim] - width, cells.shape[dim], axis=dim)
        cells = jnp.concatenate(
            [
                lax.ppermute(tail, axis, [(i, (i + 1) % count) for i in range(count)]),
                cells,
                lax.ppermute(head, axis, [((i + 1) % count, i) for i in range(count)]),
            ],
            axis=dim,
        )
    return cells


def from_behind(shard, axis, by):
    devices = lax.axis_size(axis)
    return lax.ppermute(shard, axis, [(i, (i + by) % devices) for i in range(devices)])


def pixel_grid(pixel_count):
    pixel_index = jnp.arange(pixel_count, dtype=jnp.int32)
    across = (pixel_index % IMG_W).astype(jnp.float32)
    downward = (pixel_index // IMG_W).astype(jnp.float32)
    return ((across + 0.5) / IMG_W - 0.5, (downward + 0.5 - 0.5 * IMG_H) / IMG_W)


def edge_terms(relative, target_depth, flows, weights, across, downward):
    spin_x, spin_y, spin_z, move_x, move_y, move_z = [relative[i][:, None] for i in range(6)]
    point_x = across + spin_y - spin_z * downward + move_x * target_depth
    point_y = downward + spin_z * across - spin_x + move_y * target_depth
    point_z = 1.0 + spin_x * downward - spin_y * across + move_z * target_depth
    recip_z = 1.0 / point_z
    image_u = point_x * recip_z
    image_v = point_y * recip_z
    resid_u = flows[0] - (image_u - across)
    resid_v = flows[1] - (image_v - downward)
    slope_u = recip_z * (move_x - image_u * move_z)
    slope_v = recip_z * (move_y - image_v * move_z)
    depth_recip = target_depth * recip_z
    blank_map = jnp.zeros_like(recip_z)
    jac_u = jnp.stack(
        [
            -image_u * downward * recip_z,
            (1.0 + image_u * across) * recip_z,
            -downward * recip_z,
            depth_recip,
            blank_map,
            -image_u * depth_recip,
        ]
    )
    jac_v = jnp.stack(
        [
            (-1.0 - image_v * downward) * recip_z,
            image_v * across * recip_z,
            across * recip_z,
            blank_map,
            depth_recip,
            -image_v * depth_recip,
        ]
    )
    weight_u = weights[0]
    weight_v = weights[1]
    depth_grad = weight_u * slope_u * resid_u + weight_v * slope_v * resid_v
    depth_curv = weight_u * slope_u * slope_u + weight_v * slope_v * slope_v
    scaled_u = weight_u * jac_u
    scaled_v = weight_v * jac_v
    coupling = scaled_u * slope_u + scaled_v * slope_v
    block = jnp.einsum("aep,bep->eab", scaled_u, jac_u, precision=PRECISE) + jnp.einsum(
        "aep,bep->eab", scaled_v, jac_v, precision=PRECISE
    )
    pose_grad = jnp.einsum("aep,ep->ea", scaled_u, resid_u, precision=PRECISE) + jnp.einsum(
        "aep,ep->ea", scaled_v, resid_v, precision=PRECISE
    )
    return (depth_grad, depth_curv, coupling, block, pose_grad)


def solve_frames(block_table):
    frame_count = block_table.shape[0]
    matrix = block_table[:, :36].reshape(frame_count, 6, 6).transpose(1, 2, 0)
    right_side = block_table[:, 36:].T
    factor = {}
    for i in range(6):
        for j in range(i + 1):
            element = matrix[i, j]
            if i == j:
                element = element * (1.0 + LEVENBERG) + RIDGE
            for k in range(j):
                element = element - factor[i, k] * factor[j, k]
            factor[i, j] = jnp.sqrt(element) if i == j else element / factor[j, j]
    forward = []
    for i in range(6):
        element = right_side[i]
        for k in range(i):
            element = element - factor[i, k] * forward[k]
        forward.append(element / factor[i, i])
    result = [None] * 6
    for i in reversed(range(6)):
        element = forward[i]
        for k in range(i + 1, 6):
            element = element - factor[k, i] * result[k]
        result[i] = element / factor[i, i]
    return jnp.stack(result, 1)


def spread(values):
    nearby = with_halo(values[None], (("row", 0),), 1)
    return lax.all_gather(nearby, "col", axis=1, tiled=True)


def collect(buffer):
    col_part = lax.psum_scatter(buffer, "col", scatter_dimension=1, tiled=True)
    from_next = from_behind(col_part[0], "row", -1)
    from_prev = from_behind(col_part[2], "row", 1)
    return col_part[1] + from_next + from_prev


def shards(inv_depth, rotation, translation, edge_target, flow_obs, weight):
    frames_dev, pixels = inv_depth.shape
    per_frame = edge_target.shape[1]
    edges = frames_dev * per_frame
    columns = lax.axis_size("col")
    loop_size = lax.axis_size("row")
    group_size = frames_dev * columns
    total_frames = group_size * loop_size
    my_row = lax.axis_index("row")
    first_frame = (my_row * columns + lax.axis_index("col")) * frames_dev
    targets = edge_target.reshape(edges)
    sources = first_frame + jnp.arange(edges, dtype=jnp.int32) // per_frame
    offsets = (targets // group_size - my_row + 1 + loop_size) % loop_size
    slot_index = offsets * group_size + targets % group_size
    across, downward = pixel_grid(pixels)
    pose_parts = (
        lax.all_gather(rotation, ("row", "col"), axis=1, tiled=True),
        lax.all_gather(translation, ("row", "col"), axis=1, tiled=True),
    )
    pose_all = jnp.concatenate(pose_parts, 0)
    frame_ids = jnp.arange(total_frames, dtype=jnp.int32)
    src_hot = (sources[:, None] == frame_ids[None, :]).astype(jnp.float32)
    tgt_hot = (targets[:, None] == frame_ids[None, :]).astype(jnp.float32)
    pair_hot = src_hot - tgt_hot
    relative = jnp.dot(pair_hot, pose_all.T, precision=PRECISE).T
    nearby_depth = spread(inv_depth).reshape(3 * group_size, pixels)
    target_depth = jnp.take(nearby_depth, slot_index, axis=0)
    depth_grad, depth_curv, coupling, block, pose_grad = edge_terms(
        relative,
        target_depth,
        flow_obs.reshape(2, edges, pixels),
        weight.reshape(2, edges, pixels),
        across,
        downward,
    )
    slot_hot = (jnp.arange(3 * group_size, dtype=jnp.int32)[:, None] == slot_index[None, :]).astype(
        jnp.float32
    )

    def coalesce(values):
        flat_rows = values.reshape(edges, -1)
        summed = jnp.dot(slot_hot, flat_rows, precision=PRECISE)
        return summed.reshape((3, group_size) + values.shape[1:])

    depth_sums = collect(coalesce(jnp.stack([depth_grad, depth_curv], 1)))
    grad_sum = depth_sums[:, 0]
    inverse = 1.0 / (DAMP_DEPTH + depth_sums[:, 1])
    scaled = grad_sum * inverse
    returned = spread(jnp.stack([inverse, scaled], 1)).reshape(3 * group_size, 2, pixels)
    at_edges = jnp.take(returned, slot_index, axis=0)
    reduced = block - jnp.einsum(
        "aep,bep->eab", coupling * at_edges[:, 0][None], coupling, precision=PRECISE
    )
    reduced_grad = pose_grad - jnp.einsum("aep,ep->ea", coupling, at_edges[:, 1], precision=PRECISE)
    flat_block = reduced.reshape(edges, 36)
    out_rows = jnp.concatenate([flat_block, reduced_grad], 1)
    in_rows = jnp.concatenate([flat_block, -reduced_grad], 1)
    block_table = jnp.dot(src_hot.T, out_rows, precision=PRECISE) + jnp.dot(
        tgt_hot.T, in_rows, precision=PRECISE
    )
    block_table = lax.psum(block_table, ("row", "col"))
    frame_steps = solve_frames(block_table)
    own_step = lax.dynamic_slice_in_dim(frame_steps, first_frame, frames_dev, 0)
    motion = jnp.dot(pair_hot, frame_steps, precision=PRECISE)
    correction = jnp.einsum("aep,ea->ep", coupling, motion, precision=PRECISE)
    fix_sum = collect(coalesce(correction))
    depth_next = inv_depth + (grad_sum - fix_sum) * inverse
    return (depth_next, own_step.T)


def solution(mesh):
    return jax.shard_map(
        shards,
        mesh=mesh,
        in_specs=(
            P(("row", "col"), None),
            P(None, ("row", "col")),
            P(None, ("row", "col")),
            P(("row", "col"), None),
            P(None, ("row", "col"), None, None),
            P(None, ("row", "col"), None, None),
        ),
        out_specs=(P(("row", "col"), None), P(None, ("row", "col"))),
        check_vma=False,
    )
```

profile of v0, /device:TPU:0, one launch (start us, length us, event | category | flops | bytes accessed | tf_op | source)
XLA Modules:
  0.0 454.0 jit_solution(9152022826286836492)
XLA Ops:
  8.0 5.1 %collective-permute-start.1 = (f32[1,2,3072]{2,0,1:T(1,128)S(1)}, f32[1,2,3072]{2,0,1:T(1,128)S(1)}, u32[]{:S(2)}, u32[]{:S(2)}) collective-permute-start(f32[1,2,3072]{2,0,1:T(1,128)S(1)} %broadcast_in_dim.30), channel_id=1, source_target_pairs={{8,0},{16,8},{24,16},{0,24},{9,1},{17,9},{25,17},{1,25},{10,2},{18... | collective-permute-start | bytes 73736 | tf_op jit(solution)/shard_map/ppermute | solution.py:23
  17.0 42.3 %all-gather = f32[32,2,3]{2,1,0:T(2,128)S(1)} all-gather(f32[1,2,3]{2,1,0:T(2,128)} %bitcast.512), channel_id=1, replica_groups=mesh['row'=4,'col'=8] {'row','col'}, dimensions={0}, use_global_device_ids=true | all-gather | bytes 792 | tf_op jit(solution)/shard_map/all_gather | solution.py:148
  59.4 37.0 %all-gather.1 = f32[32,2,3]{2,1,0:T(2,128)S(1)} all-gather(f32[1,2,3]{2,1,0:T(2,128)} %bitcast.513), channel_id=1, replica_groups=mesh['row'=4,'col'=8] {'row','col'}, dimensions={0}, use_global_device_ids=true | all-gather | bytes 792 | tf_op jit(solution)/shard_map/all_gather | solution.py:149
  97.3 1.8 fusion.181
  101.0 10.5 %all_gather.14 = f32[3,16,3072]{2,0,1:T(4,128)S(1)} all-gather(f32[3,2,3072]{2,0,1:T(4,128)S(1)} %pad_maximum_fusion.1), channel_id=1, replica_groups=mesh['row'=4,'col'=8] {'col'}, dimensions={1}, use_global_device_ids=true | all-gather | bytes 663552 | tf_op jit(solution)/shard_map/all_gather | solution.py:122
  112.8 2.0 multiply_dynamic-update-slice_fusion.3
  114.8 1.5 fusion.32
  116.5 1.8 fusion.17
  124.2 48.7 %all-reduce.5.cloned.1.call-done = f32[3,16,2,3072]{3,1,2,0:T(8,128)} async-done(((f32[3,16,2,3072]{3,1,2,0:T(8,128)}), f32[3,16,2,3072]{3,1,2,0:T(8,128)}) %all-reduce.5.cloned.1.call-update) | async-done | bytes 1179664
  174.0 3.3 collective-permute-start.2
  179.1 4.3 collective-permute-done.3
  184.5 2.0 collective-permute-start.4
  188.6 1.9 collective-permute-done.4
  195.0 1.9 bitcast_subtract_fusion.1
  196.9 15.1 %all-gather.4.cloned.1.call-done = f32[3,16,2,3072]{3,2,0,1:T(2,128)} async-done(((f32[3,2,2,3072]{3,2,0,1:T(2,128)}), f32[3,16,2,3072]{3,2,0,1:T(2,128)}) %all-gather.4.cloned.1.call-update) | async-done | bytes 1179664 | tf_op jit(solution)/shard_map/all_gather | solution.py:122
  212.0 1.7 copy.35
  214.6 1.9 gather_fusion.1
  218.5 9.1 %broadcast_multiply_fusion = (f32[6,48,3072]{2,1,0:T(8,128)}, f32[6,48,3072]{2,1,0:T(8,128)S(1)}, f32[6,48,3072]{2,1,0:T(8,128)}, f32[6,48,3072]{2,1,0:T(8,128)}) fusion(f32[48,3072]{1,0:T(8,128)} %bitcast.500, f32[48,3072]{1,0:T(8,128)} %get-tuple-element.58, f32[48,3072]{1,0:T(8,128)} %get-tuple-element.55, ...), kind=kLoop, calls=%fused_computation.20 | loop fusion | flops 5308416 | bytes 24182784 | tf_op jit(solution)/shard_map/mul | solution.py:183
  227.6 12.9 %fusion.2 = f32[48,1,6]{2,1,0:T(1,128)} fusion(f32[6,48,3072]{2,1,0:T(8,128)S(1)} %get-tuple-element.39, f32[48,2,3072]{2,1,0:T(2,128)S(1)} %broadcast_select_fusion), kind=kOutput, calls=%fused_computation.4 | convolution fusion | flops 10616832 | bytes 4129920 | tf_op jit(solution)/shard_map/aep,ep->ea/dot_general | solution.py:185
  241.3 18.1 %fusion.8 = f32[48,6,6]{2,1,0:T(8,128)} fusion(f32[6,48,3072]{2,1,0:T(8,128)} %get-tuple-element.41, f32[6,48,3072]{2,1,0:T(8,128)} %get-tuple-element.60), kind=kOutput, calls=%fused_computation.10 | convolution fusion | flops 63700992 | bytes 7084800 | tf_op jit(solution)/shard_map/aep,bep->eab/dot_general | solution.py:83
  259.4 12.8 %fusion.6 = f32[48,1,6]{2,1,0:T(1,128)} fusion(f32[6,48,3072]{2,1,0:T(8,128)S(1)} %copy-done.1, f32[48,3072,1]{1,0,2:T(8,128)S(1)} %bitcast.502), kind=kOutput, calls=%fused_computation.8 | convolution fusion | flops 10616832 | bytes 4129920 | tf_op jit(solution)/shard_map/aep,ep->ea/dot_general | solution.py:86
  273.0 16.7 %fusion.19 = f32[48,6,6]{2,1,0:T(8,128)S(1)} fusion(f32[48,6,6]{2,1,0:T(8,128)} %fusion.8, f32[6,48,3072]{2,1,0:T(8,128)} %multiply_dynamic-update-slice_fusion.4, f32[6,48,3072]{2,1,0:T(8,128)} %get-tuple-element.40), kind=kOutput, calls=%fused_computation.28 | convolution fusion | flops 63702720 | bytes 7091712 | tf_op jit(solution)/shard_map/aep,bep->eab/dot_general | solution.py:83
  289.7 13.0 %fusion.10 = f32[48,1,6]{2,1,0:T(1,128)} fusion(f32[6,48,3072]{2,1,0:T(8,128)S(1)} %copy-done, f32[48,3072,1]{1,0,2:T(8,128)S(1)} %bitcast.501), kind=kOutput, calls=%fused_computation.12 | convolution fusion | flops 10616832 | bytes 4129920 | tf_op jit(solution)/shard_map/aep,ep->ea/dot_general | solution.py:86
  302.6 14.9 %fusion.24 = f32[48,6,6]{2,1,0:T(8,128)} fusion(f32[48,6,6]{2,1,0:T(8,128)S(1)} %fusion.19, f32[6,48,3072]{2,1,0:T(8,128)S(1)} %get-tuple-element.39, f32[6,48,3072]{2,1,0:T(8,128)S(1)} %copy-done.2), kind=kOutput, calls=%fused_computation.29 | convolution fusion | flops 63702720 | bytes 7091712 | tf_op jit(solution)/shard_map/aep,bep->eab/dot_general | solution.py:182
  317.5 1.6 reshape.5281
  322.4 1.6 convolution_add_fusion
  323.9 39.9 %psum.7 = f32[64,42]{0,1:T(8,128)} all-reduce(f32[64,42]{0,1:T(8,128)} %convolution_add_fusion), channel_id=1, replica_groups=mesh['row'=4,'col'=8] {'row','col'}, use_global_device_ids=true, to_apply=%region_1.2 | all-reduce | flops 2688 | bytes 21504 | tf_op jit(solution)/shard_map/psum | solution.py:192
  372.1 6.0 %fusion = f32[48,1,3072]{2,1,0:T(1,128)S(1)} fusion(f32[48,6,1]{1,2,0:T(1,128)S(1)} %bitcast.509, f32[6,48,3072]{2,1,0:T(8,128)S(1)} %get-tuple-element.39), kind=kOutput, calls=%fused_computation.2 | convolution fusion | flops 10616832 | bytes 4129920 | tf_op jit(solution)/shard_map/aep,ea->ep/dot_general | solution.py:196
  379.5 56.4 %all-reduce.7.cloned.1.call-done = f32[3,16,3072]{2,1,0:T(8,128)} async-done(((f32[3,16,3072]{2,1,0:T(8,128)}), f32[3,16,3072]{2,1,0:T(8,128)}) %all-reduce.7.cloned.1.call-update) | async-done | bytes 589840
  436.8 3.3 collective-permute-start.6
  441.6 4.1 collective-permute-done.7
  445.7 1.5 fusion.45
  (117 shorter events, 44.4 us)
Async XLA Ops:
  7.2 92.5 %copy-start.21 = (u32[32]{0:T(128)S(1)}, u32[32]{0:T(128)}, u32[]{:S(2)}) copy-start(u32[32]{0:T(128)} %constant.161) | copy-start | bytes 388
  7.2 165.7 %all-reduce.5.cloned.1.call-start = ((), (), s32[]{:S(2)}) async-start(), calls=%async_computation.1 | async-start | bytes 2359296
  8.0 93.0 %collective-permute-start.1 = (f32[1,2,3072]{2,0,1:T(1,128)S(1)}, f32[1,2,3072]{2,0,1:T(1,128)S(1)}, u32[]{:S(2)}, u32[]{:S(2)}) collective-permute-start(f32[1,2,3072]{2,0,1:T(1,128)S(1)} %broadcast_in_dim.30), channel_id=1, source_target_pairs={{8,0},{16,8},{24,16},{0,24},{9,1},{17,9},{25,17},{1,25},{10,2},{18... | collective-permute-start | bytes 73736 | tf_op jit(solution)/shard_map/ppermute | solution.py:23
  13.1 87.8 %collective-permute-start = (f32[1,2,3072]{2,0,1:T(1,128)S(1)}, f32[1,2,3072]{2,0,1:T(1,128)S(1)}, u32[]{:S(2)}, u32[]{:S(2)}) collective-permute-start(f32[1,2,3072]{2,0,1:T(1,128)S(1)} %broadcast_in_dim.30), channel_id=1, source_target_pairs={{0,8},{8,16},{16,24},{24,0},{1,9},{9,17},{17,25},{25,1},{2,10},{10... | collective-permute-start | bytes 73736 | tf_op jit(solution)/shard_map/ppermute | solution.py:21
  13.9 98.0 %copy-start.20 = (s32[48]{0:T(128)}, s32[48]{0:T(128)S(1)}, u32[]{:S(2)}) copy-start(s32[48]{0:T(128)S(1)} %reshape.5243) | copy-start | bytes 580
  15.9 96.1 %copy-start.22 = (s32[48]{0:T(128)}, s32[48]{0:T(128)S(1)}, u32[]{:S(2)}) copy-start(s32[48]{0:T(128)S(1)} %fusion.82) | copy-start | bytes 580
  99.0 15.8 %copy-start.3 = (f32[1,2,24,3072]{3,2,1,0:T(8,128)}, f32[1,2,24,3072]{3,2,1,0:T(8,128)S(1)}, u32[]{:S(2)}) copy-start(f32[1,2,24,3072]{3,2,1,0:T(8,128)S(1)} %get-tuple-element.72) | copy-start | bytes 1769476
  99.0 15.8 %copy-start.4 = (f32[1,2,24,3072]{3,2,1,0:T(8,128)}, f32[1,2,24,3072]{3,2,1,0:T(8,128)S(1)}, u32[]{:S(2)}) copy-start(f32[1,2,24,3072]{3,2,1,0:T(8,128)S(1)} %get-tuple-element.73) | copy-start | bytes 1769476
  112.8 3.6 copy-start.17
  112.8 3.6 copy-start.18
  116.4 2.0 copy-start.7
  116.4 2.0 copy-start.10
  116.4 2.0 copy-start.11
  116.4 2.0 copy-start.12
  116.5 6.3 %copy-start.16 = (f32[48]{0:T(128)S(1)}, f32[48]{0:T(128)}, u32[]{:S(2)}) copy-start(f32[48]{0:T(128)} %get-tuple-element.67) | copy-start | bytes 580
  118.3 93.7 %all-gather.4.cloned.1.call-start = ((), (), s32[]{:S(2)}) async-start(), calls=%async_computation | async-start | bytes 1327104 | tf_op jit(solution)/shard_map/all_gather | solution.py:122
  119.7 66.9 %copy-start.13 = (f32[3072]{0:T(1024)S(1)}, f32[3072]{0:T(1024)}, u32[]{:S(2)}) copy-start(f32[3072]{0:T(1024)} %fusion.76) | copy-start | bytes 36868
  174.0 5.1 %collective-permute-start.2 = (f32[2,2,3072]{2,0,1:T(2,128)S(1)}, f32[2,2,3072]{2,0,1:T(2,128)S(1)}, u32[]{:S(2)}, u32[]{:S(2)}) collective-permute-start(f32[2,2,3072]{2,0,1:T(2,128)S(1)} %get-tuple-element.48), channel_id=1, source_target_pairs={{0,24},{8,0},{16,8},{24,16},{1,25},{9,1},{17,9},{25,17},{2,26},{10... | collective-permute-start | bytes 147464 | tf_op jit(solution)/shard_map/ppermute | solution.py:32
  177.3 6.1 %collective-permute-start.3 = (f32[2,2,3072]{2,0,1:T(2,128)S(1)}, f32[2,2,3072]{2,0,1:T(2,128)S(1)}, u32[]{:S(2)}, u32[]{:S(2)}) collective-permute-start(f32[2,2,3072]{2,0,1:T(2,128)S(1)} %get-tuple-element.49), channel_id=1, source_target_pairs={{0,8},{8,16},{16,24},{24,0},{1,9},{9,17},{17,25},{25,1},{2,10},{10... | collective-permute-start | bytes 147464 | tf_op jit(solution)/shard_map/ppermute | solution.py:32
  184.4 4.2 copy-start.8
  184.4 4.2 copy-start.9
  184.5 4.1 collective-permute-start.5
  184.5 5.9 %collective-permute-start.4 = (f32[1,2,2,3072]{3,1,2,0:T(2,128)S(1)}, f32[1,2,2,3072]{3,1,2,0:T(2,128)S(1)}, u32[]{:S(2)}, u32[]{:S(2)}) collective-permute-start(f32[1,2,2,3072]{3,1,2,0:T(2,128)S(1)} %maximum_bitcast_fusion.1), channel_id=1, source_target_pairs={{0,8},{8,16},{16,24},{24,0},{1,9},{9,17},{17,25},{25,1},{2,10},{10... | collective-permute-start | bytes 147464 | tf_op jit(solution)/shard_map/ppermute | solution.py:21
  191.3 244.5 %all-reduce.7.cloned.1.call-start = ((), (), s32[]{:S(2)}) async-start(), calls=%async_computation.2 | async-start | bytes 1179648
  241.3 18.1 %copy-start.1 = (f32[6,48,3072]{2,1,0:T(8,128)S(1)}, f32[6,48,3072]{2,1,0:T(8,128)}, u32[]{:S(2)}) copy-start(f32[6,48,3072]{2,1,0:T(8,128)} %get-tuple-element.41) | copy-start | bytes 10616836
  241.3 18.1 %copy-start.6 = (f32[48,3072]{1,0:T(8,128)S(1)}, f32[48,3072]{1,0:T(8,128)}, u32[]{:S(2)}) copy-start(f32[48,3072]{1,0:T(8,128)} %get-tuple-element.59) | copy-start | bytes 1769476
  273.0 16.7 %copy-start = (f32[6,48,3072]{2,1,0:T(8,128)S(1)}, f32[6,48,3072]{2,1,0:T(8,128)}, u32[]{:S(2)}) copy-start(f32[6,48,3072]{2,1,0:T(8,128)} %get-tuple-element.40) | copy-start | bytes 10616836
  273.0 16.7 %copy-start.5 = (f32[48,3072]{1,0:T(8,128)S(1)}, f32[48,3072]{1,0:T(8,128)}, u32[]{:S(2)}) copy-start(f32[48,3072]{1,0:T(8,128)} %get-tuple-element.54) | copy-start | bytes 1769476
  289.6 13.0 %copy-start.2 = (f32[6,48,3072]{2,1,0:T(8,128)S(1)}, f32[6,48,3072]{2,1,0:T(8,128)}, u32[]{:S(2)}) copy-start(f32[6,48,3072]{2,1,0:T(8,128)} %get-tuple-element.38) | copy-start | bytes 10616836
  317.5 60.6 %copy-start.19 = (s32[48]{0:T(128)S(1)}, s32[48]{0:T(128)}, u32[]{:S(2)}) copy-start(s32[48]{0:T(128)} %get-tuple-element.45) | copy-start | bytes 580
  436.8 4.8 %collective-permute-start.6 = (f32[2,3072]{1,0:T(2,128)S(1)}, f32[2,3072]{1,0:T(2,128)S(1)}, u32[]{:S(2)}, u32[]{:S(2)}) collective-permute-start(f32[2,3072]{1,0:T(2,128)S(1)} %get-tuple-element.62), channel_id=1, source_target_pairs={{0,24},{8,0},{16,8},{24,16},{1,25},{9,1},{17,9},{25,17},{2,26},{10... | collective-permute-start | bytes 73736 | tf_op jit(solution)/shard_map/ppermute | solution.py:32
  440.1 5.6 %collective-permute-start.7 = (f32[2,3072]{1,0:T(2,128)S(1)}, f32[2,3072]{1,0:T(2,128)S(1)}, u32[]{:S(2)}, u32[]{:S(2)}) collective-permute-start(f32[2,3072]{1,0:T(2,128)S(1)} %get-tuple-element.63), channel_id=1, source_target_pairs={{0,8},{8,16},{16,24},{24,0},{1,9},{9,17},{17,25},{25,1},{2,10},{10... | collective-permute-start | bytes 73736 | tf_op jit(solution)/shard_map/ppermute | solution.py:32
  (2 other events, 3.9 us)
Sparse Core Ops, SparseCore 0:
  118.4 54.4 all-reduce.4
  191.4 20.5 all-gather.3
  379.6 56.1 all-reduce.6
where the time goes:
time: 461 us; the launch traced here: 454 us
  waiting for transfers between devices  133 us (29%)
  blocking collectives  130 us (28%)
  matrix products  101 us (22%)
  other arithmetic  33.8 us (7%)
  local copies, waits for them, and re-layouts  27.4 us (6%)
  between operations  15 us (3%)
  starting transfers between devices  14.4 us (3%)
    unnamed x5, waiting for transfers between devices  105 us
    all_gather x1, blocking collectives, shards(): lax.all_gather(rotation, ('row', 'col'), axis=1, tiled=True)  42.3 us
    psum x1, blocking collectives, shards(): block_table = lax.psum(block_table, ('row', 'col'))  39.9 us
    all_gather x1, blocking collectives, shards(): lax.all_gather(translation, ('row', 'col'), axis=1, tiled=True)  37 us
    dot_general x1, matrix products, edge_terms(): jnp.einsum('aep,bep->eab', scaled_v, jac_v, precision=PRECISE)  18.1 us
    dot_general x1, matrix products, edge_terms(): jnp.einsum('aep,bep->eab', scaled_u, jac_u, precision=PRECISE)  16.7 us
    all_gather x1, waiting for transfers between devices, spread(): return lax.all_gather(nearby, 'col', axis=1, tiled=True)  15.1 us
    dot_general x1, matrix products, shards(): jnp.einsum('aep,bep->eab', coupling * at_edges[:, 0][None], coupling, pre...  14.9 us
  transfers between devices with their start and end apart: 11, of which 9 were waited for; matrix products, arithmetic and copies ran while one was open for 5% of the time, Pallas kernels for 0%

commit v1 on v0

--- a/solution.py
+++ b/solution.py
@@ -189,7 +189,8 @@
     block_table = jnp.dot(src_hot.T, out_rows, precision=PRECISE) + jnp.dot(
         tgt_hot.T, in_rows, precision=PRECISE
     )
-    block_table = lax.psum(block_table, ("row", "col"))
+    for mesh_axis in ("row", "col"):
+        block_table = lax.psum(block_table, mesh_axis)
     frame_steps = solve_frames(block_table)
     own_step = lax.dynamic_slice_in_dim(frame_steps, first_frame, frames_dev, 0)
     motion = jnp.dot(pair_hot, frame_steps, precision=PRECISE)

time: 461 us -> 461 us (level)
    psum x1 -> x2, blocking collectives: 39.9 us -> 43.7 us  [shards(): block_table = lax.psum(block_table, mesh_axis)]
where the time goes in v1:
time: 461 us; the launch traced here: 454 us
  blocking collectives  133 us (29%)
  waiting for transfers between devices  129 us (28%)
  matrix products  101 us (22%)
  other arithmetic  33.7 us (7%)
  local copies, waits for them, and re-layouts  27.4 us (6%)
  between operations  15.1 us (3%)
  starting transfers between devices  14.4 us (3%)
    unnamed x5, waiting for transfers between devices  101 us
    psum x2, blocking collectives, shards(): block_table = lax.psum(block_table, mesh_axis)  43.7 us
    all_gather x1, blocking collectives, shards(): lax.all_gather(rotation, ('row', 'col'), axis=1, tiled=True)  42.3 us
    all_gather x1, blocking collectives, shards(): lax.all_gather(translation, ('row', 'col'), axis=1, tiled=True)  37 us
    dot_general x1, matrix products, edge_terms(): jnp.einsum('aep,bep->eab', scaled_v, jac_v, precision=PRECISE)  18.1 us
    dot_general x1, matrix products, edge_terms(): jnp.einsum('aep,bep->eab', scaled_u, jac_u, precision=PRECISE)  16.7 us
    all_gather x1, waiting for transfers between devices, spread(): return lax.all_gather(nearby, 'col', axis=1, tiled=True)  15.1 us
    dot_general x1, matrix products, shards(): jnp.einsum('aep,bep->eab', coupling * at_edges[:, 0][None], coupling, pre...  14.9 us
  transfers between devices with their start and end apart: 11, of which 9 were waited for; matrix products, arithmetic and copies ran while one was open for 5% of the time, Pallas kernels for 0%

profile of v1, /device:TPU:0, one launch (start us, length us, event | category | flops | bytes accessed | tf_op | source)
XLA Modules:
  0.0 454.0 jit_solution(17753499618536430349)
XLA Ops:
  8.0 5.1 %collective-permute-start.1 = (f32[1,2,3072]{2,0,1:T(1,128)S(1)}, f32[1,2,3072]{2,0,1:T(1,128)S(1)}, u32[]{:S(2)}, u32[]{:S(2)}) collective-permute-start(f32[1,2,3072]{2,0,1:T(1,128)S(1)} %broadcast_in_dim.30), channel_id=1, source_target_pairs={{8,0},{16,8},{24,16},{0,24},{9,1},{17,9},{25,17},{1,25},{10,2},{18... | collective-permute-start | bytes 73736 | tf_op jit(solution)/shard_map/ppermute | solution.py:23
  17.0 42.3 %all-gather = f32[32,2,3]{2,1,0:T(2,128)S(1)} all-gather(f32[1,2,3]{2,1,0:T(2,128)} %bitcast.512), channel_id=1, replica_groups=mesh['row'=4,'col'=8] {'row','col'}, dimensions={0}, use_global_device_ids=true | all-gather | bytes 792 | tf_op jit(solution)/shard_map/all_gather | solution.py:148
  59.4 37.0 %all-gather.1 = f32[32,2,3]{2,1,0:T(2,128)S(1)} all-gather(f32[1,2,3]{2,1,0:T(2,128)} %bitcast.513), channel_id=1, replica_groups=mesh['row'=4,'col'=8] {'row','col'}, dimensions={0}, use_global_device_ids=true | all-gather | bytes 792 | tf_op jit(solution)/shard_map/all_gather | solution.py:149
  97.3 1.8 fusion.181
  101.1 10.5 %all_gather.14 = f32[3,16,3072]{2,0,1:T(4,128)S(1)} all-gather(f32[3,2,3072]{2,0,1:T(4,128)S(1)} %pad_maximum_fusion.1), channel_id=1, replica_groups=mesh['row'=4,'col'=8] {'col'}, dimensions={1}, use_global_device_ids=true | all-gather | bytes 663552 | tf_op jit(solution)/shard_map/all_gather | solution.py:122
  112.9 2.0 multiply_dynamic-update-slice_fusion.3
  116.6 1.8 fusion.17
  124.2 48.7 %all-reduce.5.cloned.1.call-done = f32[3,16,2,3072]{3,1,2,0:T(8,128)} async-done(((f32[3,16,2,3072]{3,1,2,0:T(8,128)}), f32[3,16,2,3072]{3,1,2,0:T(8,128)}) %all-reduce.5.cloned.1.call-update) | async-done | bytes 1179664
  174.0 3.3 collective-permute-start.2
  179.1 4.3 collective-permute-done.3
  184.6 2.0 collective-permute-start.4
  188.7 1.9 collective-permute-done.4
  195.1 1.9 bitcast_subtract_fusion.1
  197.0 15.1 %all-gather.4.cloned.1.call-done = f32[3,16,2,3072]{3,2,0,1:T(2,128)} async-done(((f32[3,2,2,3072]{3,2,0,1:T(2,128)}), f32[3,16,2,3072]{3,2,0,1:T(2,128)}) %all-gather.4.cloned.1.call-update) | async-done | bytes 1179664 | tf_op jit(solution)/shard_map/all_gather | solution.py:122
  212.1 1.7 copy.35
  214.6 1.9 gather_fusion.1
  218.6 9.1 %broadcast_multiply_fusion = (f32[6,48,3072]{2,1,0:T(8,128)}, f32[6,48,3072]{2,1,0:T(8,128)S(1)}, f32[6,48,3072]{2,1,0:T(8,128)}, f32[6,48,3072]{2,1,0:T(8,128)}) fusion(f32[48,3072]{1,0:T(8,128)} %bitcast.500, f32[48,3072]{1,0:T(8,128)} %get-tuple-element.58, f32[48,3072]{1,0:T(8,128)} %get-tuple-element.55, ...), kind=kLoop, calls=%fused_computation.20 | loop fusion | flops 5308416 | bytes 24182784 | tf_op jit(solution)/shard_map/mul | solution.py:183
  227.7 12.9 %fusion.2 = f32[48,1,6]{2,1,0:T(1,128)} fusion(f32[6,48,3072]{2,1,0:T(8,128)S(1)} %get-tuple-element.39, f32[48,2,3072]{2,1,0:T(2,128)S(1)} %broadcast_select_fusion), kind=kOutput, calls=%fused_computation.4 | convolution fusion | flops 10616832 | bytes 4129920 | tf_op jit(solution)/shard_map/aep,ep->ea/dot_general | solution.py:185
  241.4 18.1 %fusion.8 = f32[48,6,6]{2,1,0:T(8,128)} fusion(f32[6,48,3072]{2,1,0:T(8,128)} %get-tuple-element.41, f32[6,48,3072]{2,1,0:T(8,128)} %get-tuple-element.60), kind=kOutput, calls=%fused_computation.10 | convolution fusion | flops 63700992 | bytes 7084800 | tf_op jit(solution)/shard_map/aep,bep->eab/dot_general | solution.py:83
  259.4 12.8 %fusion.6 = f32[48,1,6]{2,1,0:T(1,128)} fusion(f32[6,48,3072]{2,1,0:T(8,128)S(1)} %copy-done.1, f32[48,3072,1]{1,0,2:T(8,128)S(1)} %bitcast.502), kind=kOutput, calls=%fused_computation.8 | convolution fusion | flops 10616832 | bytes 4129920 | tf_op jit(solution)/shard_map/aep,ep->ea/dot_general | solution.py:86
  273.0 16.7 %fusion.19 = f32[48,6,6]{2,1,0:T(8,128)S(1)} fusion(f32[48,6,6]{2,1,0:T(8,128)} %fusion.8, f32[6,48,3072]{2,1,0:T(8,128)} %multiply_dynamic-update-slice_fusion.4, f32[6,48,3072]{2,1,0:T(8,128)} %get-tuple-element.40), kind=kOutput, calls=%fused_computation.28 | convolution fusion | flops 63702720 | bytes 7091712 | tf_op jit(solution)/shard_map/aep,bep->eab/dot_general | solution.py:83
  289.7 12.9 %fusion.10 = f32[48,1,6]{2,1,0:T(1,128)} fusion(f32[6,48,3072]{2,1,0:T(8,128)S(1)} %copy-done, f32[48,3072,1]{1,0,2:T(8,128)S(1)} %bitcast.501), kind=kOutput, calls=%fused_computation.12 | convolution fusion | flops 10616832 | bytes 4129920 | tf_op jit(solution)/shard_map/aep,ep->ea/dot_general | solution.py:86
  302.7 14.9 %fusion.24 = f32[48,6,6]{2,1,0:T(8,128)} fusion(f32[48,6,6]{2,1,0:T(8,128)S(1)} %fusion.19, f32[6,48,3072]{2,1,0:T(8,128)S(1)} %get-tuple-element.39, f32[6,48,3072]{2,1,0:T(8,128)S(1)} %copy-done.2), kind=kOutput, calls=%fused_computation.29 | convolution fusion | flops 63702720 | bytes 7091712 | tf_op jit(solution)/shard_map/aep,bep->eab/dot_general | solution.py:182
  317.6 1.6 reshape.5281
  322.4 1.6 convolution_add_fusion
  324.0 20.2 %psum.14 = f32[64,42]{0,1:T(8,128)} all-reduce(f32[64,42]{0,1:T(8,128)} %convolution_add_fusion), channel_id=1, replica_groups=mesh['row'=4,'col'=8] {'row'}, use_global_device_ids=true, to_apply=%region_1.2 | all-reduce | flops 2688 | bytes 21504 | tf_op jit(solution)/shard_map/psum | solution.py:193
  344.1 23.5 %psum.15 = f32[64,42]{0,1:T(8,128)} all-reduce(f32[64,42]{0,1:T(8,128)} %psum.14), channel_id=1, replica_groups=mesh['row'=4,'col'=8] {'col'}, use_global_device_ids=true, to_apply=%region_2.3 | all-reduce | flops 2688 | bytes 21504 | tf_op jit(solution)/shard_map/psum | solution.py:193
  375.9 6.0 %fusion = f32[48,1,3072]{2,1,0:T(1,128)S(1)} fusion(f32[48,6,1]{1,2,0:T(1,128)S(1)} %bitcast.509, f32[6,48,3072]{2,1,0:T(8,128)S(1)} %get-tuple-element.39), kind=kOutput, calls=%fused_computation.2 | convolution fusion | flops 10616832 | bytes 4129920 | tf_op jit(solution)/shard_map/aep,ea->ep/dot_general | solution.py:197
  383.4 52.5 %all-reduce.7.cloned.1.call-done = f32[3,16,3072]{2,1,0:T(8,128)} async-done(((f32[3,16,3072]{2,1,0:T(8,128)}), f32[3,16,3072]{2,1,0:T(8,128)}) %all-reduce.7.cloned.1.call-update) | async-done | bytes 589840
  436.8 3.3 collective-permute-start.6
  441.6 4.1 collective-permute-done.7
  445.7 1.5 fusion.45
  (118 shorter events, 45.9 us)
Async XLA Ops:
  7.2 92.5 %copy-start.21 = (u32[32]{0:T(128)S(1)}, u32[32]{0:T(128)}, u32[]{:S(2)}) copy-start(u32[32]{0:T(128)} %constant.161) | copy-start | bytes 388
  7.2 165.8 %all-reduce.5.cloned.1.call-start = ((), (), s32[]{:S(2)}) async-start(), calls=%async_computation.1 | async-start | bytes 2359296
  8.0 93.1 %collective-permute-start.1 = (f32[1,2,3072]{2,0,1:T(1,128)S(1)}, f32[1,2,3072]{2,0,1:T(1,128)S(1)}, u32[]{:S(2)}, u32[]{:S(2)}) collective-permute-start(f32[1,2,3072]{2,0,1:T(1,128)S(1)} %broadcast_in_dim.30), channel_id=1, source_target_pairs={{8,0},{16,8},{24,16},{0,24},{9,1},{17,9},{25,17},{1,25},{10,2},{18... | collective-permute-start | bytes 73736 | tf_op jit(solution)/shard_map/ppermute | solution.py:23
  13.1 87.9 %collective-permute-start = (f32[1,2,3072]{2,0,1:T(1,128)S(1)}, f32[1,2,3072]{2,0,1:T(1,128)S(1)}, u32[]{:S(2)}, u32[]{:S(2)}) collective-permute-start(f32[1,2,3072]{2,0,1:T(1,128)S(1)} %broadcast_in_dim.30), channel_id=1, source_target_pairs={{0,8},{8,16},{16,24},{24,0},{1,9},{9,17},{17,25},{25,1},{2,10},{10... | collective-permute-start | bytes 73736 | tf_op jit(solution)/shard_map/ppermute | solution.py:21
  13.9 98.1 %copy-start.20 = (s32[48]{0:T(128)}, s32[48]{0:T(128)S(1)}, u32[]{:S(2)}) copy-start(s32[48]{0:T(128)S(1)} %reshape.5243) | copy-start | bytes 580
  15.9 96.2 %copy-start.22 = (s32[48]{0:T(128)}, s32[48]{0:T(128)S(1)}, u32[]{:S(2)}) copy-start(s32[48]{0:T(128)S(1)} %fusion.82) | copy-start | bytes 580
  99.0 15.9 %copy-start.3 = (f32[1,2,24,3072]{3,2,1,0:T(8,128)}, f32[1,2,24,3072]{3,2,1,0:T(8,128)S(1)}, u32[]{:S(2)}) copy-start(f32[1,2,24,3072]{3,2,1,0:T(8,128)S(1)} %get-tuple-element.72) | copy-start | bytes 1769476
  99.0 15.9 %copy-start.4 = (f32[1,2,24,3072]{3,2,1,0:T(8,128)}, f32[1,2,24,3072]{3,2,1,0:T(8,128)S(1)}, u32[]{:S(2)}) copy-start(f32[1,2,24,3072]{3,2,1,0:T(8,128)S(1)} %get-tuple-element.73) | copy-start | bytes 1769476
  112.9 3.6 copy-start.17
  112.9 3.6 copy-start.18
  116.5 2.0 copy-start.7
  116.5 2.0 copy-start.10
  116.5 2.0 copy-start.11
  116.5 2.0 copy-start.12
  116.5 6.2 %copy-start.16 = (f32[48]{0:T(128)S(1)}, f32[48]{0:T(128)}, u32[]{:S(2)}) copy-start(f32[48]{0:T(128)} %get-tuple-element.67) | copy-start | bytes 580
  118.4 93.7 %all-gather.4.cloned.1.call-start = ((), (), s32[]{:S(2)}) async-start(), calls=%async_computation | async-start | bytes 1327104 | tf_op jit(solution)/shard_map/all_gather | solution.py:122
  119.7 66.9 %copy-start.13 = (f32[3072]{0:T(1024)S(1)}, f32[3072]{0:T(1024)}, u32[]{:S(2)}) copy-start(f32[3072]{0:T(1024)} %fusion.76) | copy-start | bytes 36868
  174.0 5.1 %collective-permute-start.2 = (f32[2,2,3072]{2,0,1:T(2,128)S(1)}, f32[2,2,3072]{2,0,1:T(2,128)S(1)}, u32[]{:S(2)}, u32[]{:S(2)}) collective-permute-start(f32[2,2,3072]{2,0,1:T(2,128)S(1)} %get-tuple-element.48), channel_id=1, source_target_pairs={{0,24},{8,0},{16,8},{24,16},{1,25},{9,1},{17,9},{25,17},{2,26},{10... | collective-permute-start | bytes 147464 | tf_op jit(solution)/shard_map/ppermute | solution.py:32
  177.4 6.1 %collective-permute-start.3 = (f32[2,2,3072]{2,0,1:T(2,128)S(1)}, f32[2,2,3072]{2,0,1:T(2,128)S(1)}, u32[]{:S(2)}, u32[]{:S(2)}) collective-permute-start(f32[2,2,3072]{2,0,1:T(2,128)S(1)} %get-tuple-element.49), channel_id=1, source_target_pairs={{0,8},{8,16},{16,24},{24,0},{1,9},{9,17},{17,25},{25,1},{2,10},{10... | collective-permute-start | bytes 147464 | tf_op jit(solution)/shard_map/ppermute | solution.py:32
  184.5 4.2 copy-start.8
  184.5 4.2 copy-start.9
  184.5 4.1 collective-permute-start.5
  184.6 5.9 %collective-permute-start.4 = (f32[1,2,2,3072]{3,1,2,0:T(2,128)S(1)}, f32[1,2,2,3072]{3,1,2,0:T(2,128)S(1)}, u32[]{:S(2)}, u32[]{:S(2)}) collective-permute-start(f32[1,2,2,3072]{3,1,2,0:T(2,128)S(1)} %maximum_bitcast_fusion.1), channel_id=1, source_target_pairs={{0,8},{8,16},{16,24},{24,0},{1,9},{9,17},{17,25},{25,1},{2,10},{10... | collective-permute-start | bytes 147464 | tf_op jit(solution)/shard_map/ppermute | solution.py:21
  191.4 244.5 %all-reduce.7.cloned.1.call-start = ((), (), s32[]{:S(2)}) async-start(), calls=%async_computation.2 | async-start | bytes 1179648
  241.4 18.1 %copy-start.1 = (f32[6,48,3072]{2,1,0:T(8,128)S(1)}, f32[6,48,3072]{2,1,0:T(8,128)}, u32[]{:S(2)}) copy-start(f32[6,48,3072]{2,1,0:T(8,128)} %get-tuple-element.41) | copy-start | bytes 10616836
  241.4 18.1 %copy-start.6 = (f32[48,3072]{1,0:T(8,128)S(1)}, f32[48,3072]{1,0:T(8,128)}, u32[]{:S(2)}) copy-start(f32[48,3072]{1,0:T(8,128)} %get-tuple-element.59) | copy-start | bytes 1769476
  273.0 16.7 %copy-start = (f32[6,48,3072]{2,1,0:T(8,128)S(1)}, f32[6,48,3072]{2,1,0:T(8,128)}, u32[]{:S(2)}) copy-start(f32[6,48,3072]{2,1,0:T(8,128)} %get-tuple-element.40) | copy-start | bytes 10616836
  273.0 16.7 %copy-start.5 = (f32[48,3072]{1,0:T(8,128)S(1)}, f32[48,3072]{1,0:T(8,128)}, u32[]{:S(2)}) copy-start(f32[48,3072]{1,0:T(8,128)} %get-tuple-element.54) | copy-start | bytes 1769476
  289.7 13.0 %copy-start.2 = (f32[6,48,3072]{2,1,0:T(8,128)S(1)}, f32[6,48,3072]{2,1,0:T(8,128)}, u32[]{:S(2)}) copy-start(f32[6,48,3072]{2,1,0:T(8,128)} %get-tuple-element.38) | copy-start | bytes 10616836
  317.6 64.4 %copy-start.19 = (s32[48]{0:T(128)S(1)}, s32[48]{0:T(128)}, u32[]{:S(2)}) copy-start(s32[48]{0:T(128)} %get-tuple-element.45) | copy-start | bytes 580
  436.8 4.8 %collective-permute-start.6 = (f32[2,3072]{1,0:T(2,128)S(1)}, f32[2,3072]{1,0:T(2,128)S(1)}, u32[]{:S(2)}, u32[]{:S(2)}) collective-permute-start(f32[2,3072]{1,0:T(2,128)S(1)} %get-tuple-element.62), channel_id=1, source_target_pairs={{0,24},{8,0},{16,8},{24,16},{1,25},{9,1},{17,9},{25,17},{2,26},{10... | collective-permute-start | bytes 73736 | tf_op jit(solution)/shard_map/ppermute | solution.py:32
  440.1 5.6 %collective-permute-start.7 = (f32[2,3072]{1,0:T(2,128)S(1)}, f32[2,3072]{1,0:T(2,128)S(1)}, u32[]{:S(2)}, u32[]{:S(2)}) collective-permute-start(f32[2,3072]{1,0:T(2,128)S(1)} %get-tuple-element.63), channel_id=1, source_target_pairs={{0,8},{8,16},{16,24},{24,0},{1,9},{9,17},{17,25},{25,1},{2,10},{10... | collective-permute-start | bytes 73736 | tf_op jit(solution)/shard_map/ppermute | solution.py:32
  (2 other events, 3.9 us)
Sparse Core Ops, SparseCore 0:
  118.5 54.4 all-reduce.4
  191.5 20.5 all-gather.3
  383.5 52.3 all-reduce.6
